TPU v7x, 128 devices: a whole 4x4x4 slice. The times are simulated.
128 devices in a mesh: grp: 4 (over x_lo, core), mz: 32 (over y, x_hi, z).
Axes of the slice: x: 4 (x_hi: 2, x_lo: 2; x = x_hi * 2 + x_lo), y: 4, z: 4, core: 2. Of those that a mesh axis runs over, the one named last changes fastest.
Arguments:
- intensities: float32 [512, 8, 131072], P('grp', None, 'mz'), as said below
- sample_start: float32 [512, 256], P('grp'), as said below
- scan_start: float32 [8, 256], replicated, as said below
- mass_start: float32 [131072, 256], P('mz'), as said below
Outputs:
- sample_factor: float32 [512, 256], P('grp')
- scan_factor: float32 [8, 256], replicated
- mass_factor: float32 [131072, 256], P('mz')
Inputs may be any that keep to these rules, and one draw needn't show every extreme that they name: Measured intensities of the cohort. `sample_start`: a starting estimate of the sample factor. `scan_start`: a starting estimate of the scan factor. `mass_start`: a starting estimate of the m/z factor.
All inputs are finite; a program needn't handle non-finite values.
Results may differ from a plain program's by a relative error of at most 0.0001.
Values sent between devices are 32-bit elements; how exact they have to be, the bound alone decides.
A program may use at most 128 MiB of HBM per device.

v0:
```python
import jax
import jax.numpy as jnp
from jax import lax
from jax.sharding import PartitionSpec as P

STEPS = 2
precise = lax.Precision.HIGHEST


def frobenius(gram):
    return jnp.sqrt(jnp.sum(gram * gram) + 1e-12)


def gram_of(factor):
    return jnp.dot(factor.T, factor, precision=precise, preferred_element_type=jnp.float32)


def descend(factor, hessian, drive):
    product = jnp.dot(factor, hessian, precision=precise, preferred_element_type=jnp.float32)
    return factor - (product - drive) / frobenius(hessian)


def local(intensities, sample_start, scan_start, mass_start):
    factor_a = sample_start
    factor_b = scan_start
    factor_c = mass_start
    samples_here = intensities.shape[0]
    scans_here = intensities.shape[1]
    bins_here = intensities.shape[2]
    rank_width = factor_a.shape[1]
    unfolded = intensities.reshape(samples_here * scans_here, bins_here)
    for iteration in range(STEPS):
        gram_a = lax.psum(gram_of(factor_a), "grp")
        gram_b = gram_of(factor_b)
        gram_c = lax.psum(gram_of(factor_c), "mz")
        contracted = jnp.einsum("ijk,kr->ijr", intensities, factor_c, precision=precise)
        drive_a = lax.psum(jnp.einsum("ijr,jr->ir", contracted, factor_b, precision=precise), "mz")
        drive_b = lax.psum(
            jnp.einsum("ijr,ir->jr", contracted, factor_a, precision=precise), ("grp", "mz")
        )
        khatri_rao = (factor_a[:, None, :] * factor_b[None, :, :]).reshape(
            samples_here * scans_here, rank_width
        )
        hessian_a = gram_b * gram_c
        hessian_b = gram_a * gram_c
        hessian_c = gram_a * gram_b
        partial_c = lax.dot_general(
            unfolded,
            khatri_rao,
            (((0,), (0,)), ((), ())),
            precision=precise,
            preferred_element_type=jnp.float32,
        )
        drive_c = lax.psum(partial_c, "grp")
        new_c = descend(factor_c, hessian_c, drive_c)
        new_a = descend(factor_a, hessian_a, drive_a)
        new_b = descend(factor_b, hessian_b, drive_b)
        factor_a, factor_b, factor_c = (new_a, new_b, new_c)
    return (factor_a, factor_b, factor_c)


def solution(mesh):
    placed = (P("grp", None, "mz"), P("grp", None), P(), P("mz", None))
    return jax.shard_map(
        local,
        mesh=mesh,
        in_specs=placed,
        out_specs=(P("grp", None), P(), P("mz", None)),
        check_vma=False,
    )
```

profile of v0, /device:TPU:1, one launch (start us, length us, event | category | flops | bytes accessed | tf_op | source)
XLA Modules:
  0.0 1056.7 jit_solution(8836801280862759096)
XLA Ops:
  7.2 11.1 %fusion.53 = f32[256,256]{1,0:T(8,128)} fusion(f32[4096,256]{1,0:T(8,128)} %param.7), kind=kOutput, calls=%fused_computation.59 | convolution fusion | flops 3221225472 | bytes 4456448 | tf_op jit(solution)/shard_map/dot_general | solution.py:15
  18.3 16.7 %fusion.18 = f32[128,8,256]{2,1,0:T(8,128)S(1)} fusion(f32[128,8,4096]{2,1,0:T(8,128)} %param.4, f32[4096,256]{1,0:T(8,128)S(1)} %copy-done), kind=kOutput, calls=%fused_computation.16 | convolution fusion | flops 12884901888 | bytes 22020096 | tf_op jit(solution)/shard_map/ijk,kr->ijr/dot_general | solution.py:36
  35.0 0.3 fusion.36
  35.3 0.8 copy.26
  36.1 0.3 all-reduce.16.cloned.1.call-start
  36.5 28.8 %fusion.7 = f32[4096,256]{0,1:T(8,128)} fusion(f32[128,8,4096]{2,1,0:T(8,128)} %param.4, f32[8,256]{1,0:T(8,128)S(1)} %copy-done.6, f32[128,256]{0,1:T(8,128)S(1)} %copy.8), kind=kOutput, calls=%fused_computation.9 | convolution fusion | flops 12885164032 | bytes 21110784 | tf_op jit(solution)/shard_map/dot_general | solution.py:47
  65.3 1.1 fusion.54
  66.4 0.4 all-reduce.10.cloned.1.call-start
  66.9 5.7 copy.11
  72.6 0.3 fusion.35
  72.9 286.1 %all-reduce.12.cloned.1.call-done = (f32[128,256]{0,1:T(8,128)}, f32[256,256]{1,0:T(8,128)}) async-done(((f32[128,256]{0,1:T(8,128)}, f32[256,256]{1,0:T(8,128)}), (f32[128,256]{0,1:T(8,128)}, f32[256,256]{1,0:T(8,128)})) %all-reduce.12.cloned.1.call-update) | async-done | bytes 393232 | tf_op jit(solution)/shard_map/psum | solution.py:37
  359.0 115.0 %all-reduce.16.cloned.1.call-done = (f32[256,256]{1,0:T(8,128)}, f32[4096,256]{0,1:T(8,128)}) async-done(((f32[256,256]{1,0:T(8,128)}, f32[4096,256]{0,1:T(8,128)}), (f32[256,256]{1,0:T(8,128)}, f32[4096,256]{0,1:T(8,128)})) %all-reduce.16.cloned.1.call-update) | async-done | bytes 4456464 | tf_op jit(solution)/shard_map/psum | solution.py:33
  474.0 2.1 multiply_reduce_fusion.3
  476.8 11.9 %fusion.14 = f32[4096,256]{0,1:T(8,128)S(1)} fusion(f32[4096,256]{0,1:T(8,128)} %copy.11, f32[4096,256]{0,1:T(8,128)} %get-tuple-element.21, f32[4096,256]{1,0:T(8,128)} %param.7, f32[]{:T(128)S(6)} %sqrt.20, f32[256,256]{1,0:T(8,128)} %get-tuple-element.20, f32[256,256]{1,0:T(8,128)S(1)} %get-tuple-element.22), kind=kOutput, calls=%fused_computation.12 | convolution fusion | flops 3224436736 | bytes 17301508 | tf_op jit(solution)/shard_map/dot_general | solution.py:19
  488.8 4.3 fusion.55
  493.0 28.1 %fusion.20 = f32[128,8,256]{0,2,1:T(8,128)S(1)} fusion(f32[128,8,4096]{2,1,0:T(8,128)} %param.4, f32[4096,256]{0,1:T(8,128)S(1)} %fusion.14), kind=kOutput, calls=%fused_computation.18 | convolution fusion | flops 12884901888 | bytes 22020096 | tf_op jit(solution)/shard_map/ijk,kr->ijr/dot_general | solution.py:36
  522.5 0.6 fusion.29
  523.1 2.3 fusion.39
  525.5 66.3 %all-reduce = (f32[8,256]{1,0:T(8,128)S(1)}, f32[8,256]{1,0:T(8,128)S(1)}) all-reduce(f32[8,256]{1,0:T(8,128)S(1)} %bitcast.90, f32[8,256]{1,0:T(8,128)S(1)} %bitcast.91), channel_id=1, replica_groups=mesh['grp'=4,'mz'=32] {'grp','mz'}, use_global_device_ids=true, to_apply=%region_4.0 | all-reduce | flops 4096 | bytes 32768 | tf_op jit(solution)/shard_map/psum | solution.py:38
  591.7 0.2 fusion.34
  592.0 0.1 copy.34
  592.1 3.0 fusion.41
  595.2 29.0 %fusion.10 = f32[4096,256]{0,1:T(8,128)} fusion(f32[128,8,4096]{2,1,0:T(8,128)} %param.4, f32[8,256]{1,0:T(8,128)S(1)} %fusion.34, f32[128,256]{0,1:T(8,128)S(1)} %fusion.29), kind=kOutput, calls=%fused_computation.10 | convolution fusion | flops 12885164032 | bytes 21110784 | tf_op jit(solution)/shard_map/dot_general | solution.py:47
  624.2 1.1 fusion.56
  625.3 285.8 %all-reduce.10.cloned.1.call-done = (f32[128,256]{0,1:T(8,128)}, f32[256,256]{1,0:T(8,128)}) async-done(((f32[128,256]{0,1:T(8,128)}, f32[256,256]{1,0:T(8,128)}), (f32[128,256]{0,1:T(8,128)}, f32[256,256]{1,0:T(8,128)})) %all-reduce.10.cloned.1.call-update) | async-done | bytes 393232 | tf_op jit(solution)/shard_map/psum | solution.py:37
  911.1 114.7 %all-reduce.14.cloned.1.call-done = (f32[256,256]{1,0:T(8,128)}, f32[4096,256]{0,1:T(8,128)}) async-done(((f32[256,256]{1,0:T(8,128)}, f32[4096,256]{0,1:T(8,128)}), (f32[256,256]{1,0:T(8,128)}, f32[4096,256]{0,1:T(8,128)})) %all-reduce.14.cloned.1.call-update) | async-done | bytes 4456464 | tf_op jit(solution)/shard_map/psum | solution.py:33
  1025.8 2.1 multiply_reduce_fusion
  1029.9 1.6 fusion.26
  1031.5 0.8 copy.16
  1032.3 11.0 %fusion.16 = f32[4096,256]{0,1:T(8,128)} fusion(f32[4096,256]{0,1:T(8,128)} %copy-done.1, f32[4096,256]{0,1:T(8,128)} %get-tuple-element.19, f32[]{:T(128)S(6)} %sqrt.23, f32[256,256]{1,0:T(8,128)} %get-tuple-element.18, f32[256,256]{1,0:T(8,128)S(1)} %get-tuple-element.23), kind=kOutput, calls=%fused_computation.14 | convolution fusion | flops 3224436736 | bytes 13107204 | tf_op jit(solution)/shard_map/dot_general | solution.py:19
  1043.3 5.7 copy.17
  1048.9 0.8 fusion.31
  (26 shorter events, 0.3 us)
Async XLA Ops:
  7.2 351.9 %all-reduce.12.cloned.1.call-start = ((), (), s32[]{:S(2)}) async-start(), calls=%async_computation.1 | async-start | bytes 786432 | tf_op jit(solution)/shard_map/psum | solution.py:37
  7.2 11.1 %copy-start = (f32[4096,256]{1,0:T(8,128)S(1)}, f32[4096,256]{1,0:T(8,128)}, u32[]{:S(2)}) copy-start(f32[4096,256]{1,0:T(8,128)} %param.7) | copy-start | bytes 12582916
  18.3 16.7 %copy-start.6 = (f32[8,256]{1,0:T(8,128)S(1)}, f32[8,256]{1,0:T(8,128)}, u32[]{:S(2)}) copy-start(f32[8,256]{1,0:T(8,128)} %param.6) | copy-start | bytes 24580
  18.3 18.1 %copy-start.2 = (f32[128,256]{1,0:T(8,128)S(1)}, f32[128,256]{1,0:T(8,128)}, u32[]{:S(2)}) copy-start(f32[128,256]{1,0:T(8,128)} %param.5) | copy-start | bytes 393220
  36.1 437.9 %all-reduce.16.cloned.1.call-start = ((), (), s32[]{:S(2)}) async-start(), calls=%async_computation.3 | async-start | bytes 8912896 | tf_op jit(solution)/shard_map/psum | solution.py:33
  66.4 844.6 %all-reduce.10.cloned.1.call-start = ((), (), s32[]{:S(2)}) async-start(), calls=%async_computation | async-start | bytes 786432 | tf_op jit(solution)/shard_map/psum | solution.py:37
  488.7 4.3 copy-start.1
  493.0 29.5 %copy-start.5 = (f32[256,256]{1,0:T(8,128)S(1)}, f32[256,256]{1,0:T(8,128)}, u32[]{:S(2)}) copy-start(f32[256,256]{1,0:T(8,128)} %get-tuple-element.17) | copy-start | bytes 786436
  493.0 29.5 %copy-start.8 = (f32[128,256]{0,1:T(8,128)S(1)}, f32[128,256]{0,1:T(8,128)}, u32[]{:S(2)}) copy-start(f32[128,256]{0,1:T(8,128)} %get-tuple-element.16) | copy-start | bytes 393220
  493.0 98.7 %copy-start.3 = (f32[256,256]{1,0:T(8,128)S(1)}, f32[256,256]{1,0:T(8,128)}, u32[]{:S(2)}) copy-start(f32[256,256]{1,0:T(8,128)} %get-tuple-element.20) | copy-start | bytes 786436
  595.1 430.6 %all-reduce.14.cloned.1.call-start = ((), (), s32[]{:S(2)}) async-start(), calls=%async_computation.2 | async-start | bytes 8912896 | tf_op jit(solution)/shard_map/psum | solution.py:33
  1043.3 5.7 copy-start.4
  1043.3 5.7 copy-start.7
Sparse Core Ops, SparseCore 0:
  36.2 322.7 all-reduce.11
  362.4 111.6 all-reduce.15
  595.3 315.7 all-reduce.9
  914.1 111.6 all-reduce.13
where the time goes:
time: 1060 us
  waiting for transfers between devices  802 us (76%)
  matrix products  156 us (15%)
  blocking collectives  66.3 us (6%)
  between operations  18.5 us (2%)
  local copies, waits for them, and re-layouts  13.2 us (1%)
    psum x2, waiting for transfers between devices, local(): lax.psum(jnp.einsum('ijr,jr->ir', contracted, factor_b, precision=precise...  572 us
    psum x2, waiting for transfers between devices, local(): gram_a = lax.psum(gram_of(factor_a), 'grp')  230 us
    psum x1, blocking collectives, local(): lax.psum(jnp.einsum('ijr,ir->jr', contracted, factor_a, precision=precise...  66.3 us
    dot_general x2, matrix products, local(): lax.dot_general(unfolded, khatri_rao, (((0,), (0,)), ((), ())), precision...  57.8 us
    dot_general x2, matrix products, local(): jnp.einsum('ijk,kr->ijr', intensities, factor_c, precision=precise)  44.8 us
    dot_general x6, matrix products, descend(): jnp.dot(factor, hessian, precision=precise, preferred_element_type=jnp.fl...  26.2 us
    dot_general x6, matrix products, gram_of(): jnp.dot(factor.T, factor, precision=precise, preferred_element_type=jnp.f...  21.7 us
  transfers between devices with their start and end apart: 4, of which 4 were waited for; matrix products, arithmetic and copies ran while one was open for 6% of the time, Pallas kernels for 0%

commit v1 on v0

--- a/solution.py
+++ b/solution.py
@@ -35,9 +35,9 @@
         gram_c = lax.psum(gram_of(factor_c), "mz")
         contracted = jnp.einsum("ijk,kr->ijr", intensities, factor_c, precision=precise)
         drive_a = lax.psum(jnp.einsum("ijr,jr->ir", contracted, factor_b, precision=precise), "mz")
-        drive_b = lax.psum(
-            jnp.einsum("ijr,ir->jr", contracted, factor_a, precision=precise), ("grp", "mz")
-        )
+        original = jnp.einsum("ijr,ir->jr", contracted, factor_a, precision=precise)
+        current_block = lax.psum(original, "mz")
+        drive_b = lax.psum(current_block, "grp")
         khatri_rao = (factor_a[:, None, :] * factor_b[None, :, :]).reshape(
             samples_here * scans_here, rank_width
         )

time: 1060 us -> 1190 us (1.12)
  blocking collectives: 66.3 us -> 192 us
    psum x1 -> x2, blocking collectives: 66.3 us -> 192 us  [the longest x1 156 us: local(): current_block = lax.psum(original, 'mz')]
where the time goes in v1:
time: 1190 us; the launch traced here: 1180 us
  waiting for transfers between devices  800 us (67%)
  blocking collectives  192 us (16%)
  matrix products  156 us (13%)
  between operations  18.5 us (2%)
  local copies, waits for them, and re-layouts  13.2 us (1%)
    psum x2, waiting for transfers between devices, local(): lax.psum(jnp.einsum('ijr,jr->ir', contracted, factor_b, precision=precise...  570 us
    psum x2, waiting for transfers between devices, local(): gram_a = lax.psum(gram_of(factor_a), 'grp')  230 us
    psum x1, blocking collectives, local(): current_block = lax.psum(original, 'mz')  156 us
    dot_general x2, matrix products, local(): lax.dot_general(unfolded, khatri_rao, (((0,), (0,)), ((), ())), precision...  57.8 us
    dot_general x2, matrix products, local(): jnp.einsum('ijk,kr->ijr', intensities, factor_c, precision=precise)  44.8 us
    psum x1, blocking collectives, local(): drive_b = lax.psum(current_block, 'grp')  35.9 us
    dot_general x6, matrix products, descend(): jnp.dot(factor, hessian, precision=precise, preferred_element_type=jnp.fl...  26.2 us
  transfers between devices with their start and end apart: 4, of which 4 were waited for; matrix products, arithmetic and copies ran while one was open for 6% of the time, Pallas kernels for 0%

profile of v1, /device:TPU:1, one launch (start us, length us, event | category | flops | bytes accessed | tf_op | source)
XLA Modules:
  0.0 1180.7 jit_solution(4784915144424831025)
XLA Ops:
  7.2 11.1 fusion.53
  18.3 16.7 %fusion.18 = f32[128,8,256]{2,1,0:T(8,128)S(1)} fusion(f32[128,8,4096]{2,1,0:T(8,128)} %param.4, f32[4096,256]{1,0:T(8,128)S(1)} %copy-done), kind=kOutput, calls=%fused_computation.16 | convolution fusion | flops 12884901888 | bytes 22020096 | tf_op jit(solution)/shard_map/ijk,kr->ijr/dot_general | solution.py:36
  35.0 0.3 fusion.36
  35.3 0.8 copy.26
  36.1 0.3 all-reduce.17.cloned.1.call-start
  36.5 28.8 %fusion.7 = f32[4096,256]{0,1:T(8,128)} fusion(f32[128,8,4096]{2,1,0:T(8,128)} %param.4, f32[8,256]{1,0:T(8,128)S(1)} %copy-done.6, f32[128,256]{0,1:T(8,128)S(1)} %copy.8), kind=kOutput, calls=%fused_computation.9 | convolution fusion | flops 12885164032 | bytes 21110784 | tf_op jit(solution)/shard_map/dot_general | solution.py:47
  65.3 1.1 fusion.54
  66.4 0.4 all-reduce.11.cloned.1.call-start
  66.9 5.7 copy.11
  72.6 0.3 fusion.35
  72.9 286.1 %all-reduce.13.cloned.1.call-done = (f32[128,256]{0,1:T(8,128)}, f32[256,256]{1,0:T(8,128)}) async-done(((f32[128,256]{0,1:T(8,128)}, f32[256,256]{1,0:T(8,128)}), (f32[128,256]{0,1:T(8,128)}, f32[256,256]{1,0:T(8,128)})) %all-reduce.13.cloned.1.call-update) | async-done | bytes 393232 | tf_op jit(solution)/shard_map/psum | solution.py:37
  359.0 115.0 %all-reduce.17.cloned.1.call-done = (f32[256,256]{1,0:T(8,128)}, f32[4096,256]{0,1:T(8,128)}) async-done(((f32[256,256]{1,0:T(8,128)}, f32[4096,256]{0,1:T(8,128)}), (f32[256,256]{1,0:T(8,128)}, f32[4096,256]{0,1:T(8,128)})) %all-reduce.17.cloned.1.call-update) | async-done | bytes 4456464 | tf_op jit(solution)/shard_map/psum | solution.py:33
  474.0 2.1 multiply_reduce_fusion.3
  476.8 11.9 %fusion.14 = f32[4096,256]{0,1:T(8,128)S(1)} fusion(f32[4096,256]{0,1:T(8,128)} %copy.11, f32[4096,256]{0,1:T(8,128)} %get-tuple-element.23, f32[4096,256]{1,0:T(8,128)} %param.7, f32[]{:T(128)S(6)} %sqrt.20, f32[256,256]{1,0:T(8,128)} %get-tuple-element.22, f32[256,256]{1,0:T(8,128)S(1)} %get-tuple-element.24), kind=kOutput, calls=%fused_computation.12 | convolution fusion | flops 3224436736 | bytes 17301508 | tf_op jit(solution)/shard_map/dot_general | solution.py:19
  488.8 4.3 fusion.55
  493.0 28.1 %fusion.20 = f32[128,8,256]{0,2,1:T(8,128)S(1)} fusion(f32[128,8,4096]{2,1,0:T(8,128)} %param.4, f32[4096,256]{0,1:T(8,128)S(1)} %fusion.14), kind=kOutput, calls=%fused_computation.18 | convolution fusion | flops 12884901888 | bytes 22020096 | tf_op jit(solution)/shard_map/ijk,kr->ijr/dot_general | solution.py:36
  522.5 0.6 fusion.29
  523.1 2.3 fusion.39
  525.5 155.8 %all-reduce = (f32[8,256]{1,0:T(8,128)S(1)}, f32[8,256]{1,0:T(8,128)S(1)}) all-reduce(f32[8,256]{1,0:T(8,128)S(1)} %bitcast.90, f32[8,256]{1,0:T(8,128)S(1)} %bitcast.91), channel_id=1, replica_groups=mesh['grp'=4,'mz'=32] {'mz'}, use_global_device_ids=true, to_apply=%region_4.0 | all-reduce | flops 4096 | bytes 32768 | tf_op jit(solution)/shard_map/psum | solution.py:39
  681.3 35.9 %all-reduce.3 = (f32[8,256]{1,0:T(8,128)S(1)}, f32[8,256]{1,0:T(8,128)S(1)}) all-reduce(f32[8,256]{1,0:T(8,128)S(1)} %get-tuple-element.12, f32[8,256]{1,0:T(8,128)S(1)} %get-tuple-element.13), channel_id=1, replica_groups=mesh['grp'=4,'mz'=32] {'grp'}, use_global_device_ids=true, to_apply=%region_5.0 | all-reduce | flops 4096 | bytes 32768 | tf_op jit(solution)/shard_map/psum | solution.py:40
  717.2 0.2 fusion.34
  717.6 3.0 fusion.41
  720.6 29.0 %fusion.10 = f32[4096,256]{0,1:T(8,128)} fusion(f32[128,8,4096]{2,1,0:T(8,128)} %param.4, f32[8,256]{1,0:T(8,128)S(1)} %fusion.34, f32[128,256]{0,1:T(8,128)S(1)} %fusion.29), kind=kOutput, calls=%fused_computation.10 | convolution fusion | flops 12885164032 | bytes 21110784 | tf_op jit(solution)/shard_map/dot_general | solution.py:47
  749.7 1.1 fusion.56
  750.8 284.3 %all-reduce.11.cloned.1.call-done = (f32[128,256]{0,1:T(8,128)}, f32[256,256]{1,0:T(8,128)}) async-done(((f32[128,256]{0,1:T(8,128)}, f32[256,256]{1,0:T(8,128)}), (f32[128,256]{0,1:T(8,128)}, f32[256,256]{1,0:T(8,128)})) %all-reduce.11.cloned.1.call-update) | async-done | bytes 393232 | tf_op jit(solution)/shard_map/psum | solution.py:37
  1035.1 114.7 %all-reduce.15.cloned.1.call-done = (f32[256,256]{1,0:T(8,128)}, f32[4096,256]{0,1:T(8,128)}) async-done(((f32[256,256]{1,0:T(8,128)}, f32[4096,256]{0,1:T(8,128)}), (f32[256,256]{1,0:T(8,128)}, f32[4096,256]{0,1:T(8,128)})) %all-reduce.15.cloned.1.call-update) | async-done | bytes 4456464 | tf_op jit(solution)/shard_map/psum | solution.py:33
  1149.7 2.1 multiply_reduce_fusion
  1153.9 1.6 fusion.26
  1155.5 0.8 copy.16
  1156.2 11.0 fusion.16
  1167.2 5.7 copy.17
  1172.9 0.8 fusion.31
  (27 shorter events, 0.5 us)
Async XLA Ops:
  7.2 351.9 %all-reduce.13.cloned.1.call-start = ((), (), s32[]{:S(2)}) async-start(), calls=%async_computation.1 | async-start | bytes 786432 | tf_op jit(solution)/shard_map/psum | solution.py:37
  7.2 11.1 copy-start
  18.3 16.7 %copy-start.6 = (f32[8,256]{1,0:T(8,128)S(1)}, f32[8,256]{1,0:T(8,128)}, u32[]{:S(2)}) copy-start(f32[8,256]{1,0:T(8,128)} %param.6) | copy-start | bytes 24580
  18.3 18.1 %copy-start.2 = (f32[128,256]{1,0:T(8,128)S(1)}, f32[128,256]{1,0:T(8,128)}, u32[]{:S(2)}) copy-start(f32[128,256]{1,0:T(8,128)} %param.5) | copy-start | bytes 393220
  36.1 437.9 %all-reduce.17.cloned.1.call-start = ((), (), s32[]{:S(2)}) async-start(), calls=%async_computation.3 | async-start | bytes 8912896 | tf_op jit(solution)/shard_map/psum | solution.py:33
  66.4 968.6 %all-reduce.11.cloned.1.call-start = ((), (), s32[]{:S(2)}) async-start(), calls=%async_computation | async-start | bytes 786432 | tf_op jit(solution)/shard_map/psum | solution.py:37
  488.7 4.3 copy-start.1
  493.0 29.5 %copy-start.5 = (f32[256,256]{1,0:T(8,128)S(1)}, f32[256,256]{1,0:T(8,128)}, u32[]{:S(2)}) copy-start(f32[256,256]{1,0:T(8,128)} %get-tuple-element.17) | copy-start | bytes 786436
  493.0 29.5 %copy-start.8 = (f32[128,256]{0,1:T(8,128)S(1)}, f32[128,256]{0,1:T(8,128)}, u32[]{:S(2)}) copy-start(f32[128,256]{0,1:T(8,128)} %get-tuple-element.16) | copy-start | bytes 393220
  493.0 224.1 %copy-start.3 = (f32[256,256]{1,0:T(8,128)S(1)}, f32[256,256]{1,0:T(8,128)}, u32[]{:S(2)}) copy-start(f32[256,256]{1,0:T(8,128)} %get-tuple-element.22) | copy-start | bytes 786436
  720.6 429.1 %all-reduce.15.cloned.1.call-start = ((), (), s32[]{:S(2)}) async-start(), calls=%async_computation.2 | async-start | bytes 8912896 | tf_op jit(solution)/shard_map/psum | solution.py:33
  1167.2 5.7 copy-start.4
  1167.2 5.7 copy-start.7
Sparse Core Ops, SparseCore 0:
  36.2 322.7 all-reduce.12
  362.4 111.6 all-reduce.16
  720.7 314.3 all-reduce.10
  1038.1 111.6 all-reduce.14
